TPU v7x, 512 devices: a whole 4x4x16 slice. The times are simulated.
512 devices in a mesh: seq: 64 (over z, x), vis: 8 (over y, core).
Axes of the slice: x: 4, y: 4, z: 16, core: 2. Of those that a mesh axis runs over, the one named last changes fastest.
Arguments:
- queries: bfloat16 [16384, 4096], P('seq', 'vis'), may hold values from -120 to 120
- keys: bfloat16 [256, 8, 512], P('seq', 'vis'), may hold values from -7 to 7
- values: bfloat16 [256, 8, 512], P('seq', 'vis'), may hold values from -6 to 6
- grad_out: bfloat16 [16384, 4096], P('seq', 'vis'), may hold values from -6 to 6
- block_map: int32 [64, 32], replicated, may hold values from 0 to 255, as said below
- block_count: int32 [64], replicated, may hold values from 24 to 32, as said below
Outputs:
- grad_queries: bfloat16 [16384, 4096], P('seq', 'vis')
- log_totals: float32 [32, 16384], P('vis', 'seq')
- grad_keys: bfloat16 [256, 8, 512], P('seq', 'vis')
- grad_values: bfloat16 [256, 8, 512], P('seq', 'vis')
Inputs may be any that keep to these rules, and one draw needn't show every extreme that they name: `block_map`: block b belongs to seq index b // 4; the 32 blocks that one span names belong to 32 different seq indices. `block_count`: some span attends all 32 of its named blocks.
All inputs are finite; a program needn't handle non-finite values.
Results may differ from a plain program's by a relative error of at most 0.014.
Values may be sent and summed in bfloat16 or wider, within the bound.
A program may use at most 64 MiB of HBM per device.

v0:
```python
import math

import jax
import jax.numpy as jnp
from jax import lax
from jax.sharding import PartitionSpec as P

HEAD_DIM = 128
GROUP = 8


def contract_rows(left, right):
    return lax.dot_general(
        left, right, (((0,), (0,)), ((), ())), preferred_element_type=jnp.float32
    )


def contract_cols(left, right):
    return lax.dot_general(
        left, right, (((1,), (1,)), ((), ())), preferred_element_type=jnp.float32
    )


def add_columns(total, term, start):
    current = lax.dynamic_slice_in_dim(total, start, HEAD_DIM, 1)
    return lax.dynamic_update_slice_in_dim(total, current + term, start, 1)


def attend(queries, grad_out, key_rows, value_rows, key_live, first_head):
    score_scale = 1.0 / math.sqrt(HEAD_DIM)
    head_count = queries.shape[1] // HEAD_DIM
    query_parts, log_parts = ([], [])
    key_total = jnp.zeros(key_rows.shape, jnp.float32)
    value_total = jnp.zeros(value_rows.shape, jnp.float32)
    for head_index in range(head_count):
        low = head_index * HEAD_DIM
        high = low + HEAD_DIM
        kv_start = (first_head + head_index) // GROUP * HEAD_DIM
        q_head = queries[:, low:high]
        g_head = grad_out[:, low:high]
        k_head = lax.dynamic_slice_in_dim(key_rows, kv_start, HEAD_DIM, 1)
        v_head = lax.dynamic_slice_in_dim(value_rows, kv_start, HEAD_DIM, 1)
        scores = contract_cols(q_head, k_head) * score_scale
        scores = jnp.where(key_live[None, :], scores, -1e30)
        row_max = jnp.max(scores, axis=1)
        weights = jnp.exp(scores - row_max[:, None])
        totals = jnp.sum(weights, axis=1)
        probs_full = weights / totals[:, None]
        probs_low = probs_full.astype(jnp.bfloat16)
        context = jnp.dot(probs_low, v_head, preferred_element_type=jnp.float32)
        delta_row = jnp.sum(g_head.astype(jnp.float32) * context, axis=1)
        value_total = add_columns(value_total, contract_rows(probs_low, g_head), kv_start)
        grad_probs = contract_cols(g_head, v_head)
        grad_scores = (probs_full * (grad_probs - delta_row[:, None])).astype(jnp.bfloat16)
        query_parts.append(
            jnp.dot(grad_scores, k_head, preferred_element_type=jnp.float32) * score_scale
        )
        key_total = add_columns(
            key_total, contract_rows(grad_scores, q_head) * score_scale, kv_start
        )
        log_parts.append(row_max + jnp.log(totals))
    grad_query = jnp.concatenate(query_parts, axis=1).astype(jnp.bfloat16)
    return (grad_query, jnp.stack(log_parts, axis=0), key_total, value_total)


def local(queries, keys, values, grad_out, block_map, block_count):
    seq_count = lax.axis_size("seq")
    my_seq = lax.axis_index("seq")
    my_vis = lax.axis_index("vis")
    first_head = my_vis * (queries.shape[1] // HEAD_DIM)
    per_owner = keys.shape[0]
    most_blocks = block_map.shape[1]
    owner_seq = block_map // per_owner
    local_block = block_map % per_owner
    live_blocks = jnp.arange(most_blocks, dtype=jnp.int32)[None, :] < block_count[:, None]
    asked_here = (owner_seq == my_seq) & live_blocks
    requested = jnp.any(asked_here, axis=1)
    local_slot = jnp.sum(jnp.where(asked_here, local_block, 0), axis=1)
    my_owners = lax.dynamic_index_in_dim(owner_seq, my_seq, 0, keepdims=False)
    my_count = lax.dynamic_index_in_dim(block_count, my_seq, 0, keepdims=False)
    my_live = jnp.arange(most_blocks, dtype=jnp.int32) < my_count
    source_ids = jnp.arange(seq_count, dtype=jnp.int32)
    from_source = jnp.any((my_owners[None, :] == source_ids[:, None]) & my_live[None, :], axis=1)
    stacked = jnp.stack([keys, values])
    whole_rows = lax.all_gather(stacked, "vis", axis=2, tiled=True)
    selected = whole_rows[:, local_slot]
    fetched = lax.all_to_all(
        jnp.where(requested[None, :, None, None], selected, jnp.zeros_like(selected)),
        "seq",
        split_axis=1,
        concat_axis=1,
        tiled=True,
    )
    block_rows = fetched.shape[2]
    col_width = fetched.shape[3]
    key_live = jnp.repeat(from_source, block_rows)
    key_value_rows = fetched.reshape(2, -1, col_width)
    grad_query, log_totals, key_terms, value_terms = attend(
        queries, grad_out, key_value_rows[0], key_value_rows[1], key_live, first_head
    )
    partial_terms = jnp.stack([key_terms, value_terms]).reshape(2, -1, block_rows, col_width)
    owner_onehot = (
        requested[None, :]
        & (local_slot[None, :] == jnp.arange(per_owner, dtype=jnp.int32)[:, None])
    ).astype(jnp.float32)
    returned = lax.all_to_all(
        partial_terms.astype(jnp.bfloat16), "seq", split_axis=1, concat_axis=1, tiled=True
    ).astype(partial_terms.dtype)
    returned_flat = returned.reshape(2, seq_count, -1)
    summed = jnp.einsum("ln,tnx->tlx", owner_onehot, returned_flat, precision=lax.Precision.HIGHEST)
    grad_blocks = lax.psum_scatter(
        summed.reshape(2, per_owner, returned.shape[2], returned.shape[3]).astype(jnp.bfloat16),
        "vis",
        scatter_dimension=2,
        tiled=True,
    ).astype(jnp.float32)
    grad_blocks = grad_blocks.astype(jnp.bfloat16)
    return (grad_query, log_totals, grad_blocks[0], grad_blocks[1])


def solution(mesh):
    in_specs = (
        P("seq", "vis"),
        P("seq", "vis", None),
        P("seq", "vis", None),
        P("seq", "vis"),
        P(),
        P(),
    )
    out_specs = (P("seq", "vis"), P("vis", "seq"), P("seq", "vis", None), P("seq", "vis", None))
    return jax.shard_map(local, mesh=mesh, in_specs=in_specs, out_specs=out_specs, check_vma=False)
```

profile of v0, /device:TPU:1, one launch (start us, length us, event | category | flops | bytes accessed | tf_op | source)
XLA Modules:
  0.0 244.0 jit_solution(8980911439784200128)
XLA Ops:
  7.2 0.7 copy-done.3
  7.9 0.7 maximum_bitcast_fusion.1
  8.6 19.4 %all_gather.3 = bf16[2,4,8,512]{3,1,0,2:T(4,128)(2,1)S(1)} all-gather(bf16[2,4,1,512]{3,1,0,2:T(4,128)(2,1)S(1)} %maximum_bitcast_fusion.1), channel_id=1, replica_groups=mesh['seq'=64,'vis'=8] {'vis'}, dimensions={2}, use_global_device_ids=true | all-gather | bytes 73728 | tf_op jit(solution)/shard_map/all_gather | solution.py:85
  28.0 0.7 copy-done.2
  28.8 0.6 gather_fusion
  29.4 1.1 select_bitcast_fusion
  30.6 13.6 %all-to-all-start = ((bf16[2,64,8,512]{3,2,0,1:T(8,128)(2,1)}), bf16[2,64,8,512]{3,2,0,1:T(8,128)(2,1)S(1)}, u32[]{:S(2)}, u32[]{:S(2)}) async-start(bf16[2,64,8,512]{3,2,0,1:T(8,128)(2,1)} %select_bitcast_fusion), calls=%async_computation | async-start | bytes 2097152 | tf_op jit(solution)/shard_map/all_to_all | solution.py:87
  44.4 0.6 dynamic_slice.51
  44.9 0.2 dynamic-slice_reduce_fusion
  45.1 0.7 iota_compare_fusion.3
  46.5 50.4 %all-to-all-done = bf16[2,64,8,512]{3,2,0,1:T(8,128)(2,1)S(1)} async-done(((bf16[2,64,8,512]{3,2,0,1:T(8,128)(2,1)}), bf16[2,64,8,512]{3,2,0,1:T(8,128)(2,1)S(1)}, u32[]{:S(2)}, u32[]{:S(2)}) %all-to-all-start) | async-done | bytes 1048608 | tf_op jit(solution)/shard_map/all_to_all | solution.py:87
  97.0 0.3 fusion.117
  97.2 0.1 fusion.39
  97.4 0.3 fusion.31
  97.6 0.2 fusion.8
  97.9 0.3 fusion.118
  98.2 0.1 fusion.37
  98.3 0.3 fusion.30
  98.6 0.2 fusion.9
  98.8 0.3 fusion.119
  99.2 0.3 fusion.29
  99.5 0.2 fusion.10
  99.7 0.3 fusion.120
  100.0 0.1 fusion.33
  100.1 0.3 fusion.28
  100.4 0.2 fusion.11
  100.8 0.2 convolution_dynamic-update-slice_fusion
  101.0 0.3 fusion.15
  101.3 0.2 fusion.14
  101.6 0.2 fusion.13
  102.0 0.2 fusion.23
  102.3 0.2 fusion.22
  102.5 0.2 fusion.20
  102.8 0.2 fusion.18
  103.2 1.1 copy.46
  104.4 8.1 %all-to-all-start.1 = ((bf16[2,64,8,512]{3,2,0,1:T(8,128)(2,1)}), bf16[2,64,8,512]{3,2,0,1:T(8,128)(2,1)S(1)}, u32[]{:S(2)}, u32[]{:S(2)}) async-start(bf16[2,64,8,512]{3,2,0,1:T(8,128)(2,1)} %copy.46), calls=%async_computation.1 | async-start | bytes 2097152 | tf_op jit(solution)/shard_map/all_to_all | solution.py:106
  112.5 1.3 dynamic-slice
  113.8 0.2 fusion.27
  114.1 0.2 fusion.26
  114.3 0.2 fusion.25
  114.6 0.2 fusion.24
  114.9 48.8 %all-to-all-done.1 = bf16[2,64,8,512]{3,2,0,1:T(8,128)(2,1)S(1)} async-done(((bf16[2,64,8,512]{3,2,0,1:T(8,128)(2,1)}), bf16[2,64,8,512]{3,2,0,1:T(8,128)(2,1)S(1)}, u32[]{:S(2)}, u32[]{:S(2)}) %all-to-all-start.1) | async-done | bytes 1048608 | tf_op jit(solution)/shard_map/all_to_all | solution.py:106
  163.7 0.8 reshape.132
  164.4 1.3 convolution_convert_fusion
  165.8 0.6 pad_maximum_fusion.1
  166.4 0.8 copy.49
  167.2 68.0 %all-reduce.3.cloned.1.call-done = bf16[2,4,8,512]{3,1,2,0:T(4,128)(2,1)} async-done(((bf16[2,4,8,512]{3,1,2,0:T(4,128)(2,1)}), bf16[2,4,8,512]{3,1,2,0:T(4,128)(2,1)}) %all-reduce.3.cloned.1.call-update) | async-done | bytes 65552
  235.2 2.0 dynamic-slice_bitcast_fusion
  (37 shorter events, 1.8 us)
Async XLA Ops:
  7.2 0.7 copy-start.3
  28.0 0.7 copy-start.2
  28.0 0.7 copy-start.4
  30.6 13.6 %copy-start.1 = (bf16[256,512]{1,0:T(8,128)(2,1)S(1)}, bf16[256,512]{1,0:T(8,128)(2,1)}, u32[]{:S(2)}) copy-start(bf16[256,512]{1,0:T(8,128)(2,1)} %param.9) | copy-start | bytes 786436
  30.6 66.3 %all-to-all-start = ((bf16[2,64,8,512]{3,2,0,1:T(8,128)(2,1)}), bf16[2,64,8,512]{3,2,0,1:T(8,128)(2,1)S(1)}, u32[]{:S(2)}, u32[]{:S(2)}) async-start(bf16[2,64,8,512]{3,2,0,1:T(8,128)(2,1)} %select_bitcast_fusion), calls=%async_computation | async-start | bytes 2097152 | tf_op jit(solution)/shard_map/all_to_all | solution.py:87
  46.4 50.5 %copy-start = (bf16[256,512]{1,0:T(8,128)(2,1)S(1)}, bf16[256,512]{1,0:T(8,128)(2,1)}, u32[]{:S(2)}) copy-start(bf16[256,512]{1,0:T(8,128)(2,1)} %param.6) | copy-start | bytes 786436
  104.4 59.3 %all-to-all-start.1 = ((bf16[2,64,8,512]{3,2,0,1:T(8,128)(2,1)}), bf16[2,64,8,512]{3,2,0,1:T(8,128)(2,1)S(1)}, u32[]{:S(2)}, u32[]{:S(2)}) async-start(bf16[2,64,8,512]{3,2,0,1:T(8,128)(2,1)} %copy.46), calls=%async_computation.1 | async-start | bytes 2097152 | tf_op jit(solution)/shard_map/all_to_all | solution.py:106
  112.4 122.8 %all-reduce.3.cloned.1.call-start = ((), (), s32[]{:S(2)}) async-start(), calls=%async_computation.2 | async-start | bytes 131072
Sparse Core Ops, SparseCore 0:
  165.9 69.2 all-reduce.2
where the time goes:
time: 245 us; the launch traced here: 244 us
  waiting for transfers between devices  167 us (68%)
  starting transfers between devices  21.7 us (9%)
  blocking collectives  19.4 us (8%)
  between operations  14.4 us (6%)
  local copies, waits for them, and re-layouts  9.97 us (4%)
  matrix products  7.25 us (3%)
  other arithmetic  4.06 us (2%)
    unnamed x2, waiting for transfers between devices  68 us
    all_to_all x1, waiting for transfers between devices, local(): lax.all_to_all(jnp.where(requested[None, :, None, None], selected, jnp.ze...  50.4 us
    all_to_all x1, waiting for transfers between devices, local(): lax.all_to_all(partial_terms.astype(jnp.bfloat16), 'seq', split_axis=1, c...  48.8 us
    all_gather x1, blocking collectives, local(): whole_rows = lax.all_gather(stacked, 'vis', axis=2, tiled=True)  19.4 us
    all_to_all x1, starting transfers between devices, local(): lax.all_to_all(jnp.where(requested[None, :, None, None], selected, jnp.ze...  13.6 us
    all_to_all x1, starting transfers between devices, local(): lax.all_to_all(partial_terms.astype(jnp.bfloat16), 'seq', split_axis=1, c...  8.06 us
  transfers between devices with their start and end apart: 3, of which 3 were waited for; matrix products, arithmetic and copies ran while one was open for 2% of the time, Pallas kernels for 0%

commit v1 on v0

v1 whole, which is shorter than its diff:
```python
import math

import jax
import jax.numpy as jnp
from jax import lax
from jax.experimental import pallas as pl
from jax.experimental.pallas import tpu as pltpu
from jax.sharding import PartitionSpec as P

HEAD_DIM = 128
GROUP = 8
N_X = 4
N_CORE = 2
MESH = pl.DeviceIdType.MESH
F32 = jnp.float32
BF16 = jnp.bfloat16


def rows_cols(left, right, dims):
    return lax.dot_general(left, right, (dims, ((), ())), preferred_element_type=F32)


def kernel(
    sizes,
    q_hbm,
    g_hbm,
    k_hbm,
    v_hbm,
    map_hbm,
    count_ref,
    dq_hbm,
    log_hbm,
    dk_hbm,
    dv_hbm,
    q_buf,
    g_buf,
    dq_buf,
    log_buf,
    own_rows,
    map_buf,
    land,
    table,
    pick_t,
    pack_t,
    chosen,
    got,
    kv_buf,
    part,
    part_in,
    terms,
    terms_in,
    sums,
    fin,
    out_rows,
    local_sem,
    send_sem,
    recv_sem,
):
    n_z, n_vis, per_owner, n_named, heads = sizes
    n_plane = N_X * n_vis
    seq = lax.axis_index("seq")
    vis = lax.axis_index("vis")
    z, x = seq // N_X, seq % N_X
    y, core = vis // N_CORE, vis % N_CORE
    place = x * n_vis + vis
    block = n_vis

    def plane_peer(step):
        where = (place + step) % n_plane
        return where // n_vis, where % n_vis

    def line_peer(step):
        back = (step + 1) // 2
        ahead = n_z // 2 + back * (1 - 2 * (step % 2))
        return (z + ahead) % n_z

    partner = (seq, y * N_CORE + 1 - core)

    barrier = pltpu.get_barrier_semaphore()

    def greet_line(step, carry):
        pl.semaphore_signal(
            barrier, inc=1, device_id=(line_peer(step) * N_X + x, vis), device_id_type=MESH
        )
        return carry

    def greet_plane(step, carry):
        px, pv = plane_peer(step)
        pl.semaphore_signal(barrier, inc=1, device_id=(z * N_X + px, pv), device_id_type=MESH)
        return carry

    lax.fori_loop(0, n_z - 1, greet_line, 0)
    lax.fori_loop(1, n_plane, greet_plane, 0)

    loads = [
        pltpu.make_async_copy(k_hbm, own_rows.at[0], local_sem.at[0]),
        pltpu.make_async_copy(v_hbm, own_rows.at[1], local_sem.at[1]),
        pltpu.make_async_copy(map_hbm, map_buf, local_sem.at[2]),
        pltpu.make_async_copy(q_hbm, q_buf, local_sem.at[3]),
        pltpu.make_async_copy(g_hbm, g_buf, local_sem.at[4]),
    ]
    for load in loads:
        load.start()
    loads[2].wait()

    block_ids = map_buf[...]
    n_seq = n_z * N_X
    owner_ids = block_ids // per_owner
    slot_ids = block_ids % per_owner
    wide = n_seq * block
    keys_n = n_named * block

    def iota(shape, axis):
        return lax.broadcasted_iota(jnp.int32, shape, axis)

    sub = iota((8, n_seq), 0)
    slots = jnp.zeros((8, n_seq), F32)
    for ox in range(N_X):
        slot = jnp.sum(
            jnp.where(owner_ids == z * N_X + ox, slot_ids, 0).astype(F32), axis=0, keepdims=True
        )
        slots = jnp.where(sub == ox, jnp.broadcast_to(slot, (8, n_seq)), slots)
    spread = jnp.where(
        iota((n_seq, wide), 0) == iota((n_seq, wide), 1) // (N_X * block) * N_X + x, 1.0, 0.0
    ).astype(BF16)
    slots = rows_cols(slots.astype(BF16), spread, ((1,), (0,)))
    lane_x = iota((8, wide), 1) // block % N_X
    slot_row = jnp.sum(jnp.where(iota((8, wide), 0) == lane_x, slots, 0.0), axis=0, keepdims=True)
    lane = iota((1, wide), 1)
    target = lane % block * (N_X * per_owner) + lane // block % N_X * per_owner
    target = target + slot_row.astype(jnp.int32)
    pick_t[...] = jnp.where(iota((n_plane * per_owner, wide), 0) == target, 1.0, 0.0).astype(BF16)

    my_owner = jnp.sum(
        jnp.where(iota((n_named, n_seq), 1) == seq, owner_ids, 0).astype(F32),
        axis=1,
        keepdims=True,
    )
    owner_row = jnp.sum(
        jnp.where(
            iota((n_named, keys_n), 0) == iota((n_named, keys_n), 1) // block,
            jnp.broadcast_to(my_owner, (n_named, keys_n)),
            0.0,
        ),
        axis=0,
        keepdims=True,
    )
    target = owner_row.astype(jnp.int32) * block + iota((1, keys_n), 1) % block
    pack_t[...] = jnp.where(iota((wide, keys_n), 0) == target, 1.0, 0.0).astype(BF16)

    loads[0].wait()
    loads[1].wait()
    pl.semaphore_wait(barrier, n_z - 1 + n_plane - 1)

    def piece(py, pc):
        return own_rows.at[pc, :, pl.ds(pl.multiple_of(py * HEAD_DIM, HEAD_DIM), HEAD_DIM)]

    here = vis * N_X + x

    def send_row(step, carry):
        px, pv = plane_peer(step)
        pltpu.make_async_remote_copy(
            src_ref=piece(pv // N_CORE, pv % N_CORE),
            dst_ref=land.at[here],
            send_sem=send_sem.at[0],
            recv_sem=recv_sem.at[0],
            device_id=(z * N_X + px, pv),
            device_id_type=MESH,
        ).start()
        return carry

    lax.fori_loop(1, n_plane, send_row, 0)
    keep = pltpu.make_async_copy(piece(y, core), land.at[here], local_sem.at[0])
    keep.start()
    keep.wait()

    def wait_bytes(ref, sem):
        pltpu.make_async_copy(ref, ref, sem).wait()

    wait_bytes(land.at[pl.ds(0, n_plane - 1)], recv_sem.at[0])
    for i in range(n_plane):
        table[i * per_owner : (i + 1) * per_owner, :] = land[i].astype(F32)

    line_rows = N_X * block
    chosen[...] = (
        rows_cols(pick_t[...], table[...].astype(BF16), ((0,), (0,)))
        .astype(BF16)
        .reshape(n_z, line_rows, HEAD_DIM)
    )

    def send_line(source, target_ref, slot):
        def body(step, carry):
            pz = line_peer(step)
            pltpu.make_async_remote_copy(
                src_ref=source.at[pz],
                dst_ref=target_ref.at[z],
                send_sem=send_sem.at[slot],
                recv_sem=recv_sem.at[slot],
                device_id=(pz * N_X + x, vis),
                device_id_type=MESH,
            ).start()
            return carry

        lax.fori_loop(0, n_z - 1, body, 0)
        own = pltpu.make_async_copy(source.at[z], target_ref.at[z], local_sem.at[0])
        own.start()
        own.wait()

    send_line(chosen, got, 1)
    wait_bytes(got.at[pl.ds(0, n_z - 1)], recv_sem.at[1])

    kv_buf[core] = rows_cols(
        pack_t[...], got[...].reshape(wide, HEAD_DIM), ((0,), (0,))
    ).astype(BF16)
    swap = pltpu.make_async_remote_copy(
        src_ref=kv_buf.at[core],
        dst_ref=kv_buf.at[core],
        send_sem=send_sem.at[2],
        recv_sem=recv_sem.at[2],
        device_id=partner,
        device_id_type=MESH,
    )
    swap.start()
    loads[3].wait()
    loads[4].wait()
    swap.wait()

    k_rows = kv_buf[0]
    v_rows = kv_buf[1]
    score_scale = 1.0 / math.sqrt(HEAD_DIM)
    live = lax.broadcasted_iota(jnp.int32, (keys_n, 1), 0) < count_ref[seq] * block
    dk = jnp.zeros((keys_n, HEAD_DIM), F32)
    dv = jnp.zeros((keys_n, HEAD_DIM), F32)
    for head in range(heads):
        cols = slice(head * HEAD_DIM, (head + 1) * HEAD_DIM)
        q_head = q_buf[:, cols]
        g_head = g_buf[:, cols]
        scores = rows_cols(k_rows, q_head, ((1,), (1,))) * score_scale
        scores = jnp.where(live, scores, -1e30)
        row_max = jnp.max(scores, axis=0, keepdims=True)
        weights = jnp.exp(scores - row_max)
        totals = jnp.sum(weights, axis=0, keepdims=True)
        log_buf[head : head + 1, :] = row_max + jnp.log(totals)
        probs = weights * (1.0 / totals)
        probs_low = probs.astype(BF16)
        grad_probs = rows_cols(v_rows, g_head, ((1,), (1,)))
        delta = jnp.sum(probs_low.astype(F32) * grad_probs, axis=0, keepdims=True)
        grad_scores = (probs * (grad_probs - delta)).astype(BF16)
        dv = dv + rows_cols(probs_low, g_head, ((1,), (0,)))
        dk = dk + rows_cols(grad_scores, q_head, ((1,), (0,)))
        dq_buf[:, cols] = (rows_cols(grad_scores, k_rows, ((0,), (0,))) * score_scale).astype(BF16)
    part[0] = dk * score_scale
    part[1] = dv

    give = pltpu.make_async_remote_copy(
        src_ref=part.at[1 - core],
        dst_ref=part_in,
        send_sem=send_sem.at[3],
        recv_sem=recv_sem.at[3],
        device_id=partner,
        device_id_type=MESH,
    )
    give.start()
    stores = [
        pltpu.make_async_copy(dq_buf, dq_hbm, local_sem.at[3]),
        pltpu.make_async_copy(log_buf, log_hbm, local_sem.at[4]),
    ]
    for store in stores:
        store.start()
    give.wait()
    both = (part[core] + part_in[...]).astype(BF16)
    terms[...] = (
        rows_cols(pack_t[...], both, ((1,), (0,)))
        .astype(BF16)
        .reshape(n_z, line_rows, HEAD_DIM)
    )
    send_line(terms, terms_in, 4)
    wait_bytes(terms_in.at[pl.ds(0, n_z - 1)], recv_sem.at[4])

    line_sum = rows_cols(pick_t[...], terms_in[...].reshape(wide, HEAD_DIM), ((1,), (0,)))
    for i in range(n_plane):
        sums[i] = line_sum[i * per_owner : (i + 1) * per_owner, :]

    def send_sum(step, carry):
        px, pv = plane_peer(step)
        pltpu.make_async_remote_copy(
            src_ref=sums.at[pv * N_X + px],
            dst_ref=fin.at[place],
            send_sem=send_sem.at[5],
            recv_sem=recv_sem.at[5],
            device_id=(z * N_X + px, pv),
            device_id_type=MESH,
        ).start()
        return carry

    lax.fori_loop(1, n_plane, send_sum, 0)
    last = pltpu.make_async_copy(sums.at[here], fin.at[place], local_sem.at[0])
    last.start()
    last.wait()
    wait_bytes(fin.at[pl.ds(0, n_plane - 1)], recv_sem.at[5])
    for pv in range(n_vis):
        total = fin[pv]
        for px in range(1, N_X):
            total = total + fin[px * n_vis + pv]
        low = (pv // N_CORE) * HEAD_DIM
        out_rows[pv % N_CORE, :, low : low + HEAD_DIM] = total.astype(BF16)
    ends = [
        pltpu.make_async_copy(out_rows.at[0], dk_hbm, local_sem.at[1]),
        pltpu.make_async_copy(out_rows.at[1], dv_hbm, local_sem.at[2]),
    ]
    for end in ends:
        end.start()
    wait_bytes(land.at[pl.ds(0, n_plane - 1)], send_sem.at[0])
    wait_bytes(got.at[pl.ds(0, n_z - 1)], send_sem.at[1])
    wait_bytes(terms_in.at[pl.ds(0, n_z - 1)], send_sem.at[4])
    wait_bytes(fin.at[pl.ds(0, n_plane - 1)], send_sem.at[5])
    for store in stores + ends:
        store.wait()


def local(queries, keys, values, grad_out, block_map, block_count):
    n_seq = lax.axis_size("seq")
    n_vis = lax.axis_size("vis")
    n_z = n_seq // N_X
    per_owner = keys.shape[0]
    width = keys.shape[2]
    n_named = block_map.shape[1]
    tokens, cols = queries.shape
    heads = cols // HEAD_DIM
    n_plane = N_X * n_vis
    keys_n = n_named * n_vis
    wide = n_seq * n_vis
    line = (n_z, N_X * n_vis, HEAD_DIM)
    any_spec = pl.BlockSpec(memory_space=pl.ANY)
    dq, log_totals, dk, dv = pl.pallas_call(
        lambda *refs: kernel((n_z, n_vis, per_owner, n_named, heads), *refs),
        name="block_attention",
        out_shape=(
            jax.ShapeDtypeStruct(queries.shape, BF16),
            jax.ShapeDtypeStruct((heads, tokens), F32),
            jax.ShapeDtypeStruct((per_owner, width), BF16),
            jax.ShapeDtypeStruct((per_owner, width), BF16),
        ),
        in_specs=[any_spec] * 5 + [pl.BlockSpec(memory_space=pltpu.SMEM)],
        out_specs=(any_spec,) * 4,
        scratch_shapes=[
            pltpu.VMEM((tokens, cols), BF16),
            pltpu.VMEM((tokens, cols), BF16),
            pltpu.VMEM((tokens, cols), BF16),
            pltpu.VMEM((heads, tokens), F32),
            pltpu.VMEM((2, per_owner, width), BF16),
            pltpu.VMEM(block_map.shape[::-1], jnp.int32),
            pltpu.VMEM((n_plane, per_owner, HEAD_DIM), BF16),
            pltpu.VMEM((n_plane * per_owner, HEAD_DIM), F32),
            pltpu.VMEM((n_plane * per_owner, wide), BF16),
            pltpu.VMEM((wide, keys_n), BF16),
            pltpu.VMEM(line, BF16),
            pltpu.VMEM(line, BF16),
            pltpu.VMEM((2, keys_n, HEAD_DIM), BF16),
            pltpu.VMEM((2, keys_n, HEAD_DIM), F32),
            pltpu.VMEM((keys_n, HEAD_DIM), F32),
            pltpu.VMEM(line, BF16),
            pltpu.VMEM(line, BF16),
            pltpu.VMEM((n_plane, per_owner, HEAD_DIM), F32),
            pltpu.VMEM((n_plane, per_owner, HEAD_DIM), F32),
            pltpu.VMEM((2, per_owner, width), BF16),
            pltpu.SemaphoreType.DMA((5,)),
            pltpu.SemaphoreType.DMA((6,)),
            pltpu.SemaphoreType.DMA((6,)),
        ],
        compiler_params=pltpu.CompilerParams(collective_id=0, has_side_effects=True),
    )(
        queries,
        grad_out,
        keys.reshape(per_owner, width),
        values.reshape(per_owner, width),
        block_map.T,
        block_count,
    )
    return (dq, log_totals, dk.reshape(keys.shape), dv.reshape(values.shape))


def solution(mesh):
    in_specs = (
        P("seq", "vis"),
        P("seq", "vis", None),
        P("seq", "vis", None),
        P("seq", "vis"),
        P(),
        P(),
    )
    out_specs = (P("seq", "vis"), P("vis", "seq"), P("seq", "vis", None), P("seq", "vis", None))
    return jax.shard_map(local, mesh=mesh, in_specs=in_specs, out_specs=out_specs, check_vma=False)
```

time: 245 us -> 55.7 us (0.23)
  waiting for transfers between devices: 167 us -> 0 us
  Pallas kernels: 0 us -> 51.2 us
  starting transfers between devices: 21.7 us -> 0 us
  blocking collectives: 19.4 us -> 0 us
  between operations: 14.4 us -> 0.65 us
  matrix products: 7.25 us -> 0 us
  local copies, waits for them, and re-layouts: 9.97 us -> 3.62 us
  other arithmetic: 4.06 us -> 0 us
    all_to_all x2 -> x0, waiting for transfers between devices: 99.2 us -> none  [the longest x1 50.4 us: local(): lax.all_to_all(jnp.where(requested[None, :, None, None], selected, jnp.ze...]
    unnamed x2 -> x0, waiting for transfers between devices: 68 us -> none
    pallas_call x0 -> x1, Pallas kernels: none -> 51.2 us  [local(): pl.pallas_call(lambda *refs: kernel((n_z, n_vis, per_owner, n_named, head...]
    all_to_all x2 -> x0, starting transfers between devices: 21.6 us -> none  [the longest x1 13.6 us: local(): lax.all_to_all(jnp.where(requested[None, :, None, None], selected, jnp.ze...]
    all_gather x1 -> x0, blocking collectives: 19.4 us -> none  [local(): whole_rows = lax.all_gather(stacked, 'vis', axis=2, tiled=True)]
    dot_general x25 -> x0, matrix products: 7.25 us -> none  [the longest x8 2.03 us: contract_cols(): lax.dot_general(left, right, (((1,), (1,)), ((), ())), preferred_element_...]
  transfers between devices with their start and end apart: 3 -> 0, of which waited for: 3 -> 0; matrix products, arithmetic and copies ran while one was open for 2% -> 0% of each run, Pallas kernels for 0% -> 0%
where the time goes in v1:
time: 55.7 us; the launch traced here: 55.5 us
  Pallas kernels  51.2 us (92%)
  local copies, waits for them, and re-layouts  3.62 us (6%)
  between operations  0.65 us (1%)
    pallas_call x1, Pallas kernels, local(): pl.pallas_call(lambda *refs: kernel((n_z, n_vis, per_owner, n_named, head...  51.2 us
    unnamed x10, local copies, waits for them, and re-layouts  3.62 us

profile of v1, /device:TPU:1, one launch (start us, length us, event | category | flops | bytes accessed | tf_op | source)
XLA Modules:
  0.0 55.5 jit_solution(13999256890819003866)
XLA Ops:
  0.6 51.2 %block_attention.1 = (bf16[256,512]{1,0:T(8,128)(2,1)}, f32[4,256]{1,0:T(4,128)}, bf16[4,512]{1,0:T(4,128)(2,1)}, bf16[4,512]{1,0:T(4,128)(2,1)}) custom-call(bf16[256,512]{1,0:T(8,128)(2,1)} %refs_0_.1, bf16[256,512]{1,0:T(8,128)(2,1)} %refs_1_.1, bf16[4,512]{1,0:T(4,128)(2,1)} %bitcast.6, bf16[4,512]{1,0:T(4,128)(2,1)} %bitcast.7, s32[32,64]{1,0:T(8,128)} %bitcast.5, ...), custom_call_target="tpu_custom_call" | custom-call | tf_op jit(solution)/shard_map/block_attention/pallas_call | solution.py:335
  51.9 0.0 copy-start.2
  51.9 1.7 %copy.14 = bf16[256,512]{1,0:T(8,128)(2,1)} copy(bf16[256,512]{1,0:T(8,128)(2,1)} %get-tuple-element.16) | data formatting | bytes 524288
  53.6 0.0 copy-done.2
  53.6 0.0 copy-start.1
  53.6 0.6 %copy.15 = f32[4,256]{1,0:T(4,128)} copy(f32[4,256]{1,0:T(4,128)S(1)} %copy-done.2) | data formatting | bytes 8192
  54.2 0.1 copy-done.1
  54.2 0.0 copy-start
  54.3 0.6 %copy.16 = bf16[4,1,512]{2,0,1:T(4,128)(2,1)} copy(bf16[4,1,512]{2,0,1:T(4,128)(2,1)S(1)} %bitcast.9) | data formatting | bytes 8192
  54.8 0.1 copy-done
  54.9 0.6 %copy.17 = bf16[4,1,512]{2,0,1:T(4,128)(2,1)} copy(bf16[4,1,512]{2,0,1:T(4,128)(2,1)S(1)} %bitcast.8) | data formatting | bytes 8192
Async XLA Ops:
  51.9 1.7 %copy-start.2 = (f32[4,256]{1,0:T(4,128)S(1)}, f32[4,256]{1,0:T(4,128)}, u32[]{:S(2)}) copy-start(f32[4,256]{1,0:T(4,128)} %get-tuple-element.17) | copy-start | bytes 12292
  53.6 0.7 %copy-start.1 = (bf16[4,512]{1,0:T(4,128)(2,1)S(1)}, bf16[4,512]{1,0:T(4,128)(2,1)}, u32[]{:S(2)}) copy-start(bf16[4,512]{1,0:T(4,128)(2,1)} %get-tuple-element.10) | copy-start | bytes 12292
  54.2 0.7 %copy-start = (bf16[4,512]{1,0:T(4,128)(2,1)S(1)}, bf16[4,512]{1,0:T(4,128)(2,1)}, u32[]{:S(2)}) copy-start(bf16[4,512]{1,0:T(4,128)(2,1)} %get-tuple-element.11) | copy-start | bytes 12292

commit v2 on v1

v2 whole, which is shorter than its diff:
```python
import math

import jax
import jax.numpy as jnp
from jax import lax
from jax.experimental import pallas as pl
from jax.experimental.pallas import tpu as pltpu
from jax.sharding import PartitionSpec as P

HEAD_DIM = 128
GROUP = 8
N_X = 4
N_CORE = 2
CHUNKS = 4
MESH = pl.DeviceIdType.MESH
F32 = jnp.float32
BF16 = jnp.bfloat16


def rows_cols(left, right, dims):
    return lax.dot_general(left, right, (dims, ((), ())), preferred_element_type=F32)


def iota(shape, axis):
    return lax.broadcasted_iota(jnp.int32, shape, axis)


def mod(a, n):
    return lax.rem(a, jnp.int32(n))


def div(a, n):
    return lax.div(a, jnp.int32(n))


def kernel(
    sizes,
    q_hbm,
    g_hbm,
    k_hbm,
    v_hbm,
    map_hbm,
    count_ref,
    dq_ref,
    log_ref,
    out_rows,
    q_buf,
    g_buf,
    own_rows,
    map_buf,
    land,
    table,
    pick_t,
    pack_t,
    chosen,
    got,
    kv_buf,
    part,
    part_in,
    terms,
    terms_in,
    sums,
    fin,
    local_sem,
    send_sem,
    recv_sem,
    ready_sem,
):
    n_z, n_vis, per_owner, n_named, heads = sizes
    n_plane = N_X * n_vis
    n_chip_y = n_vis // N_CORE
    seq = lax.axis_index("seq")
    vis = lax.axis_index("vis")
    z, x = div(seq, N_X), mod(seq, N_X)
    y, core = div(vis, N_CORE), mod(vis, N_CORE)
    block = n_vis
    n_seq = n_z * N_X
    wide = n_seq * block
    keys_n = n_named * block
    line_rows = N_X * block

    half = n_z // 2
    order = [
        (half + (p + 1) // 2 * (1 - 2 * (p % 2))) % n_z for p in range(n_z)
    ]
    place_of = {d: p for p, d in enumerate(order)}
    line_seq = [mod(z + d, n_z) * N_X + x for d in range(n_z)]
    plane_seq = [z * N_X + mod(x + d, N_X) for d in range(N_X)]
    plane_vis = [mod(vis + d, n_vis) for d in range(n_vis)]
    far_x = sorted(range(N_X), key=lambda d: -min(d, N_X - d))
    far_v = sorted(range(n_vis), key=lambda d: -min(d, n_vis - d))
    plane = [(dx, dv) for dx in far_x for dv in far_v if dx or dv]
    partner = (seq, y * N_CORE + 1 - core)

    barrier = pltpu.get_barrier_semaphore()

    def greet(device):
        pl.semaphore_signal(barrier, inc=1, device_id=device, device_id_type=MESH)

    for d in order[:-1]:
        greet((line_seq[d], y * N_CORE + 1))
    chip_vis = [mod(y + d, n_chip_y) * N_CORE for d in range(n_chip_y)]
    for dx in far_x:
        for dy in range(n_chip_y):
            if dx or dy:
                greet((plane_seq[dx], chip_vis[dy]))
    greet(partner)

    loads = [
        pltpu.make_async_copy(k_hbm, own_rows.at[0], local_sem.at[0]),
        pltpu.make_async_copy(v_hbm, own_rows.at[1], local_sem.at[1]),
        pltpu.make_async_copy(map_hbm, map_buf, local_sem.at[2]),
        pltpu.make_async_copy(q_hbm, q_buf, local_sem.at[3]),
        pltpu.make_async_copy(g_hbm, g_buf, local_sem.at[4]),
    ]
    for load in loads:
        load.start()

    def wait_bytes(ref, sem):
        pltpu.make_async_copy(ref, ref, sem).wait()

    loads[0].wait()
    loads[1].wait()

    @pl.when(core == 0)
    def _():
        pl.semaphore_wait(barrier, n_plane - 1)
        pl.semaphore_signal(ready_sem, inc=1, device_id=partner, device_id_type=MESH)

    @pl.when(core == 1)
    def _():
        pl.semaphore_wait(ready_sem, 1)

    def piece(where):
        low = pl.multiple_of(div(where, N_CORE) * HEAD_DIM, HEAD_DIM)
        return own_rows.at[mod(where, N_CORE), :, pl.ds(low, HEAD_DIM)]

    pieces = [piece(where) for where in plane_vis]
    for dx, dv in plane:
        slot = (n_vis - dv) % n_vis * N_X + (N_X - dx) % N_X
        pltpu.make_async_remote_copy(
            src_ref=pieces[dv],
            dst_ref=land.at[slot],
            send_sem=send_sem.at[0],
            recv_sem=recv_sem.at[0],
            device_id=(plane_seq[dx], plane_vis[dv]),
            device_id_type=MESH,
        ).start()

    loads[2].wait()
    block_ids = map_buf[...]
    owner_ids = div(block_ids, per_owner)
    slot_ids = mod(block_ids, per_owner)
    sub = iota((8, n_seq), 0)
    slots = jnp.zeros((8, n_seq), F32)
    for ox in range(N_X):
        slot = jnp.sum(
            jnp.where(owner_ids == z * N_X + ox, slot_ids, 0).astype(F32), axis=0, keepdims=True
        )
        slots = jnp.where(sub == ox, jnp.broadcast_to(slot, (8, n_seq)), slots)
    lane = iota((1, wide), 1)
    lane_p = div(lane, N_X * block)
    lane_d = half + div(lane_p + 1, 2) * (1 - 2 * mod(lane_p, 2))
    lane_span = mod(z + lane_d, n_z) * N_X + x
    lane_x = mod(div(lane, block), N_X)
    spread = jnp.where(iota((n_seq, wide), 0) == lane_span, 1.0, 0.0).astype(BF16)
    slots = rows_cols(slots.astype(BF16), spread, ((1,), (0,)))
    slot_row = jnp.sum(jnp.where(iota((8, wide), 0) == lane_x, slots, 0.0), axis=0, keepdims=True)
    target = mod(mod(lane, block) + n_vis - vis, n_vis) * (N_X * per_owner)
    target = target + mod(lane_x + N_X - x, N_X) * per_owner + slot_row.astype(jnp.int32)
    pick_t[...] = jnp.where(iota((n_plane * per_owner, wide), 0) == target, 1.0, 0.0).astype(BF16)

    my_owner = jnp.sum(
        jnp.where(iota((n_named, n_seq), 1) == seq, owner_ids, 0).astype(F32),
        axis=1,
        keepdims=True,
    )
    owner_row = jnp.sum(
        jnp.where(
            iota((n_named, keys_n), 0) == div(iota((n_named, keys_n), 1), block),
            jnp.broadcast_to(my_owner, (n_named, keys_n)),
            0.0,
        ),
        axis=0,
        keepdims=True,
    ).astype(jnp.int32)
    away = mod(div(owner_row, N_X) + n_z - z, n_z) - half
    owner_p = jnp.where(away >= 0, 2 * away, -2 * away - 1)
    target = (owner_p * N_X + mod(owner_row, N_X)) * block + mod(iota((1, keys_n), 1), block)
    pack_t[...] = jnp.where(iota((wide, keys_n), 0) == target, 1.0, 0.0).astype(BF16)

    @pl.when(core == 1)
    def _():
        pl.semaphore_wait(barrier, N_CORE * (n_z - 1) + 1)
        pl.semaphore_signal(ready_sem, inc=1, device_id=partner, device_id_type=MESH)

    @pl.when(core == 0)
    def _():
        pl.semaphore_wait(ready_sem, 1)

    wait_bytes(land.at[pl.ds(1, n_plane - 1)], recv_sem.at[0])
    table[0:per_owner, :] = own_rows[
        core, :, pl.ds(pl.multiple_of(y * HEAD_DIM, HEAD_DIM), HEAD_DIM)
    ].astype(F32)
    for i in range(1, n_plane):
        table[i * per_owner : (i + 1) * per_owner, :] = land[i].astype(F32)

    per_chunk = n_z // CHUNKS

    def send_line(make_chunk, source, target_ref, index):
        for chunk in range(CHUNKS):
            first = chunk * per_chunk
            rows = make_chunk(first * line_rows, (first + per_chunk) * line_rows)
            rows = rows.astype(BF16).reshape(per_chunk, line_rows, HEAD_DIM)
            source[first : first + per_chunk] = rows
            for p in range(first, first + per_chunk):
                d = order[p]
                if d == 0:
                    target_ref[p] = rows[p - first]
                    continue
                pltpu.make_async_remote_copy(
                    src_ref=source.at[p],
                    dst_ref=target_ref.at[place_of[(n_z - d) % n_z]],
                    send_sem=send_sem.at[index],
                    recv_sem=recv_sem.at[index],
                    device_id=(line_seq[d], vis),
                    device_id_type=MESH,
                ).start()

    rows_in = table[...].astype(BF16)
    send_line(
        lambda low, high: rows_cols(pick_t[:, low:high], rows_in, ((0,), (0,))), chosen, got, 1
    )
    wait_bytes(got.at[pl.ds(0, n_z - 1)], recv_sem.at[1])

    kv_buf[core] = rows_cols(
        pack_t[...], got[...].reshape(wide, HEAD_DIM), ((0,), (0,))
    ).astype(BF16)
    swap = pltpu.make_async_remote_copy(
        src_ref=kv_buf.at[core],
        dst_ref=kv_buf.at[core],
        send_sem=send_sem.at[2],
        recv_sem=recv_sem.at[2],
        device_id=partner,
        device_id_type=MESH,
    )
    swap.start()
    loads[3].wait()
    loads[4].wait()
    swap.wait()

    k_rows = kv_buf[0]
    v_rows = kv_buf[1]
    score_scale = 1.0 / math.sqrt(HEAD_DIM)
    live = iota((keys_n, 1), 0) < count_ref[seq] * block
    dk = jnp.zeros((keys_n, HEAD_DIM), F32)
    dv = jnp.zeros((keys_n, HEAD_DIM), F32)
    for head in range(heads):
        cols = slice(head * HEAD_DIM, (head + 1) * HEAD_DIM)
        q_head = q_buf[:, cols]
        g_head = g_buf[:, cols]
        scores = rows_cols(k_rows, q_head, ((1,), (1,))) * score_scale
        scores = jnp.where(live, scores, -1e30)
        row_max = jnp.max(scores, axis=0, keepdims=True)
        weights = jnp.exp(scores - row_max)
        totals = jnp.sum(weights, axis=0, keepdims=True)
        log_ref[head : head + 1, :] = row_max + jnp.log(totals)
        probs = weights * (1.0 / totals)
        probs_low = probs.astype(BF16)
        grad_probs = rows_cols(v_rows, g_head, ((1,), (1,)))
        delta = jnp.sum(probs_low.astype(F32) * grad_probs, axis=0, keepdims=True)
        grad_scores = (probs * (grad_probs - delta)).astype(BF16)
        dv = dv + rows_cols(probs_low, g_head, ((1,), (0,)))
        dk = dk + rows_cols(grad_scores, q_head, ((1,), (0,)))
        dq_ref[:, cols] = (rows_cols(grad_scores, k_rows, ((0,), (0,))) * score_scale).astype(BF16)
    part[0] = dk * score_scale
    part[1] = dv

    give = pltpu.make_async_remote_copy(
        src_ref=part.at[1 - core],
        dst_ref=part_in,
        send_sem=send_sem.at[3],
        recv_sem=recv_sem.at[3],
        device_id=partner,
        device_id_type=MESH,
    )
    give.start()
    give.wait()
    both = (part[core] + part_in[...]).astype(BF16)
    send_line(
        lambda low, high: rows_cols(pack_t[low:high, :], both, ((1,), (0,))), terms, terms_in, 4
    )
    wait_bytes(terms_in.at[pl.ds(0, n_z - 1)], recv_sem.at[4])

    line_sum = rows_cols(pick_t[...], terms_in[...].reshape(wide, HEAD_DIM), ((1,), (0,)))
    for i in range(1, n_plane):
        sums[i] = line_sum[i * per_owner : (i + 1) * per_owner, :]
    fin[0, vis] = line_sum[0:per_owner, :]
    for dx, dv_step in plane:
        pltpu.make_async_remote_copy(
            src_ref=sums.at[dv_step * N_X + dx],
            dst_ref=fin.at[(N_X - dx) % N_X, vis],
            send_sem=send_sem.at[5],
            recv_sem=recv_sem.at[5],
            device_id=(plane_seq[dx], plane_vis[dv_step]),
            device_id_type=MESH,
        ).start()
    wait_bytes(sums.at[pl.ds(1, n_plane - 1)], recv_sem.at[5])
    for pv in range(n_vis):
        total = fin[0, pv]
        for px in range(1, N_X):
            total = total + fin[px, pv]
        low = (pv // N_CORE) * HEAD_DIM
        out_rows[pv % N_CORE, :, low : low + HEAD_DIM] = total.astype(BF16)
    wait_bytes(land.at[pl.ds(1, n_plane - 1)], send_sem.at[0])
    wait_bytes(got.at[pl.ds(0, n_z - 1)], send_sem.at[1])
    wait_bytes(terms_in.at[pl.ds(0, n_z - 1)], send_sem.at[4])
    wait_bytes(sums.at[pl.ds(1, n_plane - 1)], send_sem.at[5])


def write_out(dq_ref, log_ref, rows_ref, dq_hbm, log_hbm, dk_hbm, dv_hbm, sem):
    copies = [
        pltpu.make_async_copy(dq_ref, dq_hbm, sem.at[0]),
        pltpu.make_async_copy(log_ref, log_hbm, sem.at[1]),
        pltpu.make_async_copy(rows_ref.at[0], dk_hbm, sem.at[2]),
        pltpu.make_async_copy(rows_ref.at[1], dv_hbm, sem.at[3]),
    ]
    for copy in copies:
        copy.start()
    for copy in copies:
        copy.wait()


def local(queries, keys, values, grad_out, block_map, block_count):
    n_seq = lax.axis_size("seq")
    n_vis = lax.axis_size("vis")
    n_z = n_seq // N_X
    per_owner = keys.shape[0]
    width = keys.shape[2]
    n_named = block_map.shape[1]
    tokens, cols = queries.shape
    heads = cols // HEAD_DIM
    n_plane = N_X * n_vis
    keys_n = n_named * n_vis
    wide = n_seq * n_vis
    line = (n_z, N_X * n_vis, HEAD_DIM)
    any_spec = pl.BlockSpec(memory_space=pl.ANY)
    vmem_spec = pl.BlockSpec(memory_space=pltpu.VMEM)
    results = pl.pallas_call(
        lambda *refs: kernel((n_z, n_vis, per_owner, n_named, heads), *refs),
        name="block_attention",
        out_shape=(
            pltpu.VMEM(queries.shape, BF16),
            pltpu.VMEM((heads, tokens), F32),
            pltpu.VMEM((2, per_owner, width), BF16),
        ),
        in_specs=[any_spec] * 5 + [pl.BlockSpec(memory_space=pltpu.SMEM)],
        out_specs=(vmem_spec,) * 3,
        scratch_shapes=[
            pltpu.VMEM((tokens, cols), BF16),
            pltpu.VMEM((tokens, cols), BF16),
            pltpu.VMEM((2, per_owner, width), BF16),
            pltpu.VMEM(block_map.shape[::-1], jnp.int32),
            pltpu.VMEM((n_plane, per_owner, HEAD_DIM), BF16),
            pltpu.VMEM((n_plane * per_owner, HEAD_DIM), F32),
            pltpu.VMEM((n_plane * per_owner, wide), BF16),
            pltpu.VMEM((wide, keys_n), BF16),
            pltpu.VMEM(line, BF16),
            pltpu.VMEM(line, BF16),
            pltpu.VMEM((2, keys_n, HEAD_DIM), BF16),
            pltpu.VMEM((2, keys_n, HEAD_DIM), F32),
            pltpu.VMEM((keys_n, HEAD_DIM), F32),
            pltpu.VMEM(line, BF16),
            pltpu.VMEM(line, BF16),
            pltpu.VMEM((n_plane, per_owner, HEAD_DIM), F32),
            pltpu.VMEM((N_X, n_vis, per_owner, HEAD_DIM), F32),
            pltpu.SemaphoreType.DMA((5,)),
            pltpu.SemaphoreType.DMA((6,)),
            pltpu.SemaphoreType.DMA((6,)),
            pltpu.SemaphoreType.REGULAR,
        ],
        compiler_params=pltpu.CompilerParams(collective_id=0, has_side_effects=True),
    )(
        queries,
        grad_out,
        keys.reshape(per_owner, width),
        values.reshape(per_owner, width),
        block_map.T,
        block_count,
    )
    dq, log_totals, dk, dv = pl.pallas_call(
        write_out,
        name="write_out",
        out_shape=(
            jax.ShapeDtypeStruct(queries.shape, BF16),
            jax.ShapeDtypeStruct((heads, tokens), F32),
            jax.ShapeDtypeStruct((per_owner, width), BF16),
            jax.ShapeDtypeStruct((per_owner, width), BF16),
        ),
        in_specs=[vmem_spec] * 3,
        out_specs=(any_spec,) * 4,
        scratch_shapes=[pltpu.SemaphoreType.DMA((4,))],
    )(*[pltpu.with_memory_space_constraint(r, pltpu.VMEM) for r in results])
    return (dq, log_totals, dk.reshape(keys.shape), dv.reshape(values.shape))


def solution(mesh):
    in_specs = (
        P("seq", "vis"),
        P("seq", "vis", None),
        P("seq", "vis", None),
        P("seq", "vis"),
        P(),
        P(),
    )
    out_specs = (P("seq", "vis"), P("vis", "seq"), P("seq", "vis", None), P("seq", "vis", None))
    return jax.shard_map(local, mesh=mesh, in_specs=in_specs, out_specs=out_specs, check_vma=False)
```

time: 55.7 us -> 50 us (0.90)
  local copies, waits for them, and re-layouts: 3.62 us -> 0 us
  Pallas kernels: 51.2 us -> 49.2 us
    unnamed x10 -> x0, local copies, waits for them, and re-layouts: 3.62 us -> none
    pallas_call x1, Pallas kernels: 51.2 us -> 48.5 us  [local(): pl.pallas_call(lambda *refs: kernel((n_z, n_vis, per_owner, n_named, head...]
    pallas_call x0 -> x1, Pallas kernels: none -> 0.75 us  [local(): pl.pallas_call(write_out, name='write_out', out_shape=(jax.ShapeDtypeStru...]
where the time goes in v2:
time: 50 us; the launch traced here: 49.9 us
  Pallas kernels  49.2 us (98%)
  between operations  0.64 us (1%)
    pallas_call x1, Pallas kernels, local(): pl.pallas_call(lambda *refs: kernel((n_z, n_vis, per_owner, n_named, head...  48.5 us

profile of v2, /device:TPU:1, one launch (start us, length us, event | category | flops | bytes accessed | tf_op | source)
XLA Modules:
  0.0 49.9 jit_solution(8172502036911122540)
XLA Ops:
  0.6 48.5 %block_attention.1 = (bf16[256,512]{1,0:T(8,128)(2,1)S(1)}, f32[4,256]{1,0:T(4,128)S(1)}, bf16[2,4,512]{2,1,0:T(4,128)(2,1)S(1)}) custom-call(bf16[256,512]{1,0:T(8,128)(2,1)} %refs_0_.1, bf16[256,512]{1,0:T(8,128)(2,1)} %refs_1_.1, bf16[4,512]{1,0:T(4,128)(2,1)} %bitcast.6, bf16[4,512]{1,0:T(4,128)(2,1)} %bitcast.7, s32[32,64]{1,0:T(8,128)} %bitcast.5, ...), custom_call_target="tpu_custom_call" | custom-call | tf_op jit(solution)/shard_map/block_attention/pallas_call | solution.py:349
  49.1 0.7 %write_out.1 = (bf16[256,512]{1,0:T(8,128)(2,1)}, f32[4,256]{1,0:T(4,128)}, bf16[4,512]{1,0:T(4,128)(2,1)}, bf16[4,512]{1,0:T(4,128)(2,1)}) custom-call(bf16[256,512]{1,0:T(8,128)(2,1)S(1)} %get-tuple-element.11.dq_ref, f32[4,256]{1,0:T(4,128)S(1)} %get-tuple-element.12.log_ref, bf16[2,4,512]{2,1,0:T(4,128)(2,1)S(1)} %get-tuple-element.13.rows_ref), custom_call_target="tpu_custom_call" | custom-call | tf_op jit(solution)/shard_map/write_out/pallas_call | solution.py:391

commit v3 on v2

--- a/solution.py
+++ b/solution.py
@@ -40,14 +40,16 @@
     k_hbm,
     v_hbm,
     map_hbm,
-    count_ref,
+    count_hbm,
     dq_ref,
     log_ref,
     out_rows,
-    q_buf,
-    g_buf,
+    qg_buf,
     own_rows,
     map_buf,
+    count_buf,
+    first,
+    ds_buf,
     land,
     table,
     pick_t,
@@ -92,6 +94,17 @@
     plane = [(dx, dv) for dx in far_x for dv in far_v if dx or dv]
     partner = (seq, y * N_CORE + 1 - core)
 
+    loads = [
+        pltpu.make_async_copy(k_hbm, own_rows.at[0], local_sem.at[0]),
+        pltpu.make_async_copy(v_hbm, own_rows.at[1], local_sem.at[1]),
+        pltpu.make_async_copy(map_hbm, map_buf, local_sem.at[2]),
+        pltpu.make_async_copy(q_hbm, qg_buf.at[0], local_sem.at[3]),
+        pltpu.make_async_copy(g_hbm, qg_buf.at[1], local_sem.at[4]),
+        pltpu.make_async_copy(count_hbm, count_buf, local_sem.at[5]),
+    ]
+    for load in loads:
+        load.start()
+
     barrier = pltpu.get_barrier_semaphore()
 
     def greet(device):
@@ -105,16 +118,6 @@
             if dx or dy:
                 greet((plane_seq[dx], chip_vis[dy]))
     greet(partner)
-
-    loads = [
-        pltpu.make_async_copy(k_hbm, own_rows.at[0], local_sem.at[0]),
-        pltpu.make_async_copy(v_hbm, own_rows.at[1], local_sem.at[1]),
-        pltpu.make_async_copy(map_hbm, map_buf, local_sem.at[2]),
-        pltpu.make_async_copy(q_hbm, q_buf, local_sem.at[3]),
-        pltpu.make_async_copy(g_hbm, g_buf, local_sem.at[4]),
-    ]
-    for load in loads:
-        load.start()
 
     def wait_bytes(ref, sem):
         pltpu.make_async_copy(ref, ref, sem).wait()
@@ -148,6 +151,7 @@
         ).start()
 
     loads[2].wait()
+    loads[5].wait()
     block_ids = map_buf[...]
     owner_ids = div(block_ids, per_owner)
     slot_ids = mod(block_ids, per_owner)
@@ -247,32 +251,39 @@
     swap.start()
     loads[3].wait()
     loads[4].wait()
+
+    def products(half):
+        rows = kv_buf[half]
+        for head in range(heads):
+            cols = slice(head * HEAD_DIM, (head + 1) * HEAD_DIM)
+            first[half, head] = rows_cols(rows, qg_buf[half, :, cols], ((1,), (1,)))
+
+    products(core)
     swap.wait()
-
-    k_rows = kv_buf[0]
-    v_rows = kv_buf[1]
+    products(1 - core)
+
     score_scale = 1.0 / math.sqrt(HEAD_DIM)
-    live = iota((keys_n, 1), 0) < count_ref[seq] * block
+    my_count = jnp.sum(
+        jnp.where(iota((1, n_seq), 1) == seq, count_buf[...], 0).astype(F32), axis=1, keepdims=True
+    )
+    live = iota((keys_n, 1), 0) < (my_count * block).astype(jnp.int32)
     dk = jnp.zeros((keys_n, HEAD_DIM), F32)
     dv = jnp.zeros((keys_n, HEAD_DIM), F32)
     for head in range(heads):
         cols = slice(head * HEAD_DIM, (head + 1) * HEAD_DIM)
-        q_head = q_buf[:, cols]
-        g_head = g_buf[:, cols]
-        scores = rows_cols(k_rows, q_head, ((1,), (1,))) * score_scale
-        scores = jnp.where(live, scores, -1e30)
+        scores = jnp.where(live, first[0, head] * score_scale, -1e30)
         row_max = jnp.max(scores, axis=0, keepdims=True)
         weights = jnp.exp(scores - row_max)
         totals = jnp.sum(weights, axis=0, keepdims=True)
         log_ref[head : head + 1, :] = row_max + jnp.log(totals)
         probs = weights * (1.0 / totals)
         probs_low = probs.astype(BF16)
-        grad_probs = rows_cols(v_rows, g_head, ((1,), (1,)))
+        grad_probs = first[1, head]
         delta = jnp.sum(probs_low.astype(F32) * grad_probs, axis=0, keepdims=True)
         grad_scores = (probs * (grad_probs - delta)).astype(BF16)
-        dv = dv + rows_cols(probs_low, g_head, ((1,), (0,)))
-        dk = dk + rows_cols(grad_scores, q_head, ((1,), (0,)))
-        dq_ref[:, cols] = (rows_cols(grad_scores, k_rows, ((0,), (0,))) * score_scale).astype(BF16)
+        ds_buf[head] = grad_scores
+        dv = dv + rows_cols(probs_low, qg_buf[1, :, cols], ((1,), (0,)))
+        dk = dk + rows_cols(grad_scores, qg_buf[0, :, cols], ((1,), (0,)))
     part[0] = dk * score_scale
     part[1] = dv
 
@@ -290,6 +301,10 @@
     send_line(
         lambda low, high: rows_cols(pack_t[low:high, :], both, ((1,), (0,))), terms, terms_in, 4
     )
+    for head in range(heads):
+        cols = slice(head * HEAD_DIM, (head + 1) * HEAD_DIM)
+        dq = rows_cols(ds_buf[head], kv_buf[0], ((0,), (0,)))
+        dq_ref[:, cols] = (dq * score_scale).astype(BF16)
     wait_bytes(terms_in.at[pl.ds(0, n_z - 1)], recv_sem.at[4])
 
     line_sum = rows_cols(pick_t[...], terms_in[...].reshape(wide, HEAD_DIM), ((1,), (0,)))
@@ -354,13 +369,15 @@
             pltpu.VMEM((heads, tokens), F32),
             pltpu.VMEM((2, per_owner, width), BF16),
         ),
-        in_specs=[any_spec] * 5 + [pl.BlockSpec(memory_space=pltpu.SMEM)],
+        in_specs=[any_spec] * 6,
         out_specs=(vmem_spec,) * 3,
         scratch_shapes=[
-            pltpu.VMEM((tokens, cols), BF16),
-            pltpu.VMEM((tokens, cols), BF16),
+            pltpu.VMEM((2, tokens, cols), BF16),
             pltpu.VMEM((2, per_owner, width), BF16),
             pltpu.VMEM(block_map.shape[::-1], jnp.int32),
+            pltpu.VMEM((1, n_seq), jnp.int32),
+            pltpu.VMEM((2, heads, keys_n, tokens), F32),
+            pltpu.VMEM((heads, keys_n, tokens), BF16),
             pltpu.VMEM((n_plane, per_owner, HEAD_DIM), BF16),
             pltpu.VMEM((n_plane * per_owner, HEAD_DIM), F32),
             pltpu.VMEM((n_plane * per_owner, wide), BF16),
@@ -374,7 +391,7 @@
             pltpu.VMEM(line, BF16),
             pltpu.VMEM((n_plane, per_owner, HEAD_DIM), F32),
             pltpu.VMEM((N_X, n_vis, per_owner, HEAD_DIM), F32),
-            pltpu.SemaphoreType.DMA((5,)),
+            pltpu.SemaphoreType.DMA((6,)),
             pltpu.SemaphoreType.DMA((6,)),
             pltpu.SemaphoreType.DMA((6,)),
             pltpu.SemaphoreType.REGULAR,
@@ -386,7 +403,7 @@
         keys.reshape(per_owner, width),
         values.reshape(per_owner, width),
         block_map.T,
-        block_count,
+        block_count.reshape(1, n_seq),
     )
     dq, log_totals, dk, dv = pl.pallas_call(
         write_out,

time: 50 us -> 49 us (0.980)
  Pallas kernels: 49.2 us -> 48.2 us
    pallas_call x1, Pallas kernels: 48.5 us -> 47.4 us  [local(): pl.pallas_call(lambda *refs: kernel((n_z, n_vis, per_owner, n_named, head...]
where the time goes in v3:
time: 49 us; the launch traced here: 48.8 us
  Pallas kernels  48.2 us (98%)
  between operations  0.64 us (1%)
    pallas_call x1, Pallas kernels, local(): pl.pallas_call(lambda *refs: kernel((n_z, n_vis, per_owner, n_named, head...  47.4 us

profile of v3, /device:TPU:1, one launch (start us, length us, event | category | flops | bytes accessed | tf_op | source)
XLA Modules:
  0.0 48.8 jit_solution(224763874384423855)
XLA Ops:
  0.6 47.4 %block_attention.1 = (bf16[256,512]{1,0:T(8,128)(2,1)S(1)}, f32[4,256]{1,0:T(4,128)S(1)}, bf16[2,4,512]{2,1,0:T(4,128)(2,1)S(1)}) custom-call(bf16[256,512]{1,0:T(8,128)(2,1)} %refs_0_.1, bf16[256,512]{1,0:T(8,128)(2,1)} %refs_1_.1, bf16[4,512]{1,0:T(4,128)(2,1)} %bitcast.7, bf16[4,512]{1,0:T(4,128)(2,1)} %bitcast.8, s32[32,64]{1,0:T(8,128)} %bitcast.6, ...), custom_call_target="tpu_custom_call" | custom-call | tf_op jit(solution)/shard_map/block_attention/pallas_call | solution.py:364
  48.1 0.7 %write_out.1 = (bf16[256,512]{1,0:T(8,128)(2,1)}, f32[4,256]{1,0:T(4,128)}, bf16[4,512]{1,0:T(4,128)(2,1)}, bf16[4,512]{1,0:T(4,128)(2,1)}) custom-call(bf16[256,512]{1,0:T(8,128)(2,1)S(1)} %get-tuple-element.11.dq_ref, f32[4,256]{1,0:T(4,128)S(1)} %get-tuple-element.12.log_ref, bf16[2,4,512]{2,1,0:T(4,128)(2,1)S(1)} %get-tuple-element.13.rows_ref), custom_call_target="tpu_custom_call" | custom-call | tf_op jit(solution)/shard_map/write_out/pallas_call | solution.py:408

commit v4 on v3

--- a/solution.py
+++ b/solution.py
@@ -49,7 +49,7 @@
     map_buf,
     count_buf,
     first,
-    ds_buf,
+    left,
     land,
     table,
     pick_t,
@@ -266,29 +266,31 @@
     my_count = jnp.sum(
         jnp.where(iota((1, n_seq), 1) == seq, count_buf[...], 0).astype(F32), axis=1, keepdims=True
     )
-    live = iota((keys_n, 1), 0) < (my_count * block).astype(jnp.int32)
-    dk = jnp.zeros((keys_n, HEAD_DIM), F32)
-    dv = jnp.zeros((keys_n, HEAD_DIM), F32)
+    sure = n_named * 3 // 4 * block
+    live = iota((keys_n - sure, 1), 0) + sure < (my_count * block).astype(jnp.int32)
+    factor = score_scale / math.log(2.0)
+    other = 1 - core
+    given = jnp.zeros((keys_n, HEAD_DIM), F32)
     for head in range(heads):
         cols = slice(head * HEAD_DIM, (head + 1) * HEAD_DIM)
-        scores = jnp.where(live, first[0, head] * score_scale, -1e30)
+        scores = jnp.concatenate(
+            [first[0, head, :sure], jnp.where(live, first[0, head, sure:], -1e30)], axis=0
+        )
         row_max = jnp.max(scores, axis=0, keepdims=True)
-        weights = jnp.exp(scores - row_max)
+        weights = jnp.exp2((scores - row_max) * factor)
         totals = jnp.sum(weights, axis=0, keepdims=True)
-        log_ref[head : head + 1, :] = row_max + jnp.log(totals)
+        log_ref[head : head + 1, :] = row_max * score_scale + jnp.log(totals)
         probs = weights * (1.0 / totals)
         probs_low = probs.astype(BF16)
         grad_probs = first[1, head]
         delta = jnp.sum(probs_low.astype(F32) * grad_probs, axis=0, keepdims=True)
-        grad_scores = (probs * (grad_probs - delta)).astype(BF16)
-        ds_buf[head] = grad_scores
-        dv = dv + rows_cols(probs_low, qg_buf[1, :, cols], ((1,), (0,)))
-        dk = dk + rows_cols(grad_scores, qg_buf[0, :, cols], ((1,), (0,)))
-    part[0] = dk * score_scale
-    part[1] = dv
-
+        left[0, head] = (probs * (grad_probs - delta)).astype(BF16)
+        left[1, head] = probs_low
+        given = given + rows_cols(left[other, head], qg_buf[other, :, cols], ((1,), (0,)))
+
+    part[...] = (given * jnp.where(core == 1, score_scale, 1.0)).astype(BF16)
     give = pltpu.make_async_remote_copy(
-        src_ref=part.at[1 - core],
+        src_ref=part,
         dst_ref=part_in,
         send_sem=send_sem.at[3],
         recv_sem=recv_sem.at[3],
@@ -296,14 +298,19 @@
         device_id_type=MESH,
     )
     give.start()
+    kept = jnp.zeros((keys_n, HEAD_DIM), F32)
+    for head in range(heads):
+        cols = slice(head * HEAD_DIM, (head + 1) * HEAD_DIM)
+        kept = kept + rows_cols(left[core, head], qg_buf[core, :, cols], ((1,), (0,)))
+    kept = kept * jnp.where(core == 0, score_scale, 1.0)
     give.wait()
-    both = (part[core] + part_in[...]).astype(BF16)
+    both = (kept + part_in[...].astype(F32)).astype(BF16)
     send_line(
         lambda low, high: rows_cols(pack_t[low:high, :], both, ((1,), (0,))), terms, terms_in, 4
     )
     for head in range(heads):
         cols = slice(head * HEAD_DIM, (head + 1) * HEAD_DIM)
-        dq = rows_cols(ds_buf[head], kv_buf[0], ((0,), (0,)))
+        dq = rows_cols(left[0, head], kv_buf[0], ((0,), (0,)))
         dq_ref[:, cols] = (dq * score_scale).astype(BF16)
     wait_bytes(terms_in.at[pl.ds(0, n_z - 1)], recv_sem.at[4])
 
@@ -377,7 +384,7 @@
             pltpu.VMEM(block_map.shape[::-1], jnp.int32),
             pltpu.VMEM((1, n_seq), jnp.int32),
             pltpu.VMEM((2, heads, keys_n, tokens), F32),
-            pltpu.VMEM((heads, keys_n, tokens), BF16),
+            pltpu.VMEM((2, heads, keys_n, tokens), BF16),
             pltpu.VMEM((n_plane, per_owner, HEAD_DIM), BF16),
             pltpu.VMEM((n_plane * per_owner, HEAD_DIM), F32),
             pltpu.VMEM((n_plane * per_owner, wide), BF16),
@@ -385,8 +392,8 @@
             pltpu.VMEM(line, BF16),
             pltpu.VMEM(line, BF16),
             pltpu.VMEM((2, keys_n, HEAD_DIM), BF16),
-            pltpu.VMEM((2, keys_n, HEAD_DIM), F32),
-            pltpu.VMEM((keys_n, HEAD_DIM), F32),
+            pltpu.VMEM((keys_n, HEAD_DIM), BF16),
+            pltpu.VMEM((keys_n, HEAD_DIM), BF16),
             pltpu.VMEM(line, BF16),
             pltpu.VMEM(line, BF16),
             pltpu.VMEM((n_plane, per_owner, HEAD_DIM), F32),

time: 49 us -> 48.9 us (level)
  no operation moved by 1% of the time
where the time goes in v4:
time: 48.9 us; the launch traced here: 48.7 us
  Pallas kernels  48.1 us (98%)
  between operations  0.64 us (1%)
    pallas_call x1, Pallas kernels, local(): pl.pallas_call(lambda *refs: kernel((n_z, n_vis, per_owner, n_named, head...  47.4 us

profile of v4, /device:TPU:1, one launch (start us, length us, event | category | flops | bytes accessed | tf_op | source)
XLA Modules:
  0.0 48.7 jit_solution(2496952183626814755)
XLA Ops:
  0.6 47.4 %block_attention.1 = (bf16[256,512]{1,0:T(8,128)(2,1)S(1)}, f32[4,256]{1,0:T(4,128)S(1)}, bf16[2,4,512]{2,1,0:T(4,128)(2,1)S(1)}) custom-call(bf16[256,512]{1,0:T(8,128)(2,1)} %refs_0_.1, bf16[256,512]{1,0:T(8,128)(2,1)} %refs_1_.1, bf16[4,512]{1,0:T(4,128)(2,1)} %bitcast.7, bf16[4,512]{1,0:T(4,128)(2,1)} %bitcast.8, s32[32,64]{1,0:T(8,128)} %bitcast.6, ...), custom_call_target="tpu_custom_call" | custom-call | tf_op jit(solution)/shard_map/block_attention/pallas_call | solution.py:371
  48.0 0.7 %write_out.1 = (bf16[256,512]{1,0:T(8,128)(2,1)}, f32[4,256]{1,0:T(4,128)}, bf16[4,512]{1,0:T(4,128)(2,1)}, bf16[4,512]{1,0:T(4,128)(2,1)}) custom-call(bf16[256,512]{1,0:T(8,128)(2,1)S(1)} %get-tuple-element.11.dq_ref, f32[4,256]{1,0:T(4,128)S(1)} %get-tuple-element.12.log_ref, bf16[2,4,512]{2,1,0:T(4,128)(2,1)S(1)} %get-tuple-element.13.rows_ref), custom_call_target="tpu_custom_call" | custom-call | tf_op jit(solution)/shard_map/write_out/pallas_call | solution.py:415
